TPU v7x, 32 devices: a whole 2x2x4 slice. The times are simulated.
32 devices in a mesh: dp: 8 (over z, x), tensor: 4 (over y, core).
Axes of the slice: x: 2, y: 2, z: 4, core: 2. Of those that a mesh axis runs over, the one named last changes fastest.
Arguments:
- tokens: bfloat16 [16384, 1024], P(('dp', 'tensor')), may hold values from -6 to 6
- cotangent: bfloat16 [16384, 1024], P(('dp', 'tensor')), may hold values from -6 to 6
- lengths: int32 [8, 16], P('dp'), may hold values from 1 to 256, 2048 in all within a row
- qkv_master: float32 [1024, 3, 1024], P('dp', None, 'tensor'), may hold values from -0.1875 to 0.1875
- qkv_first: float32 [1024, 3, 1024], P('dp', None, 'tensor'), may hold values from -0.00015258789 to 0.00015258789
- qkv_second: float32 [1024, 3, 1024], P('dp', None, 'tensor'), may hold values from 2.9798684e-11 to 4.7677895e-10
- out_master: float32 [1024, 1024], P(('tensor', 'dp')), may hold values from -1 to 1
- out_first: float32 [1024, 1024], P(('tensor', 'dp')), may hold values from -9.1552734e-05 to 9.1552734e-05
- out_second: float32 [1024, 1024], P(('tensor', 'dp')), may hold values from 5.959737e-12 to 9.535579e-11
- in_master: float32 [1024, 2, 4096], P('dp', None, 'tensor'), may hold values from -0.1875 to 0.1875
- in_first: float32 [1024, 2, 4096], P('dp', None, 'tensor'), may hold values from -0.00015258789 to 0.00015258789
- in_second: float32 [1024, 2, 4096], P('dp', None, 'tensor'), may hold values from 2.9798684e-11 to 4.7677895e-10
- down_master: float32 [4096, 1024], P(('tensor', 'dp')), may hold values from -0.09375 to 0.09375
- down_first: float32 [4096, 1024], P(('tensor', 'dp')), may hold values from -0.00015258789 to 0.00015258789
- down_second: float32 [4096, 1024], P(('tensor', 'dp')), may hold values from 2.9798684e-11 to 4.7677895e-10
- norm_gains: float32 [2, 1024], replicated, may hold values from 0.2 to 2.8
- gain_first: float32 [2, 1024], replicated, may hold values from -0.00061035156 to 0.00061035156
- gain_second: float32 [2, 1024], replicated, may hold values from 4.7677895e-10 to 7.628463e-09
Outputs:
- layer_out: bfloat16 [16384, 1024], P(('dp', 'tensor'))
- input_grad: float32 [16384, 1024], P(('dp', 'tensor'))
- qkv_grad: float32 [1024, 3, 1024], P('dp', None, 'tensor')
- qkv_new: float32 [1024, 3, 1024], P('dp', None, 'tensor')
- qkv_first_new: float32 [1024, 3, 1024], P('dp', None, 'tensor')
- qkv_second_new: float32 [1024, 3, 1024], P('dp', None, 'tensor')
- out_grad: float32 [1024, 1024], P(('tensor', 'dp'))
- out_new: float32 [1024, 1024], P(('tensor', 'dp'))
- out_first_new: float32 [1024, 1024], P(('tensor', 'dp'))
- out_second_new: float32 [1024, 1024], P(('tensor', 'dp'))
- in_grad: float32 [1024, 2, 4096], P('dp', None, 'tensor')
- in_new: float32 [1024, 2, 4096], P('dp', None, 'tensor')
- in_first_new: float32 [1024, 2, 4096], P('dp', None, 'tensor')
- in_second_new: float32 [1024, 2, 4096], P('dp', None, 'tensor')
- down_grad: float32 [4096, 1024], P(('tensor', 'dp'))
- down_new: float32 [4096, 1024], P(('tensor', 'dp'))
- down_first_new: float32 [4096, 1024], P(('tensor', 'dp'))
- down_second_new: float32 [4096, 1024], P(('tensor', 'dp'))
- gain_grad: float32 [2, 1024], replicated
- gain_new: float32 [2, 1024], replicated
- gain_first_new: float32 [2, 1024], replicated
- gain_second_new: float32 [2, 1024], replicated
- grad_norm: float32 [], replicated
Inputs may be any that keep to these rules, and one draw needn't show every extreme that they name: Each row's 16 window lengths are positive, add up to 2048, and the longest is 256.
All inputs are finite; a program needn't handle non-finite values.
Results may differ from a plain program's by a relative error of at most 0.024.
Values may be sent and summed in bfloat16 or wider, within the bound.
No kernel may reach another device: no remote copies, remote signals or barrier semaphores. Data moves between devices by JAX's collectives and lax.ppermute only.
A program may use at most 192 MiB of HBM per device.

v0:
```python
from functools import partial
import math
import jax
import jax.numpy as jnp
from jax import lax
from jax.sharding import PartitionSpec as P

D = 1024
HEADS = 16
HEAD_DIM = 64
FF = 4096
ROW = 2048
STEP = 5
eps_norm = 1e-05
beta_one = 0.9
beta_two = 0.999
learn_rate = 0.05
gain_rate = 0.6
weight_decay = 0.1
adam_eps = 1e-08
max_norm = 1.0


def layer_norm(values, gain):
    centre = values - jnp.mean(values, axis=-1, keepdims=True)
    spread = jnp.mean(centre * centre, axis=-1, keepdims=True)
    return centre * lax.rsqrt(spread + eps_norm) * gain


def row_layout(lengths):
    seg_ends = jnp.cumsum(lengths, axis=-1)
    places = jnp.arange(ROW, dtype=jnp.int32)
    passed = (places[:, None] >= seg_ends[..., None, :]).astype(jnp.int32)
    segment = jnp.sum(passed, axis=-1)
    offset = places - jnp.sum(passed * lengths[..., None, :], axis=-1)
    return (segment, offset)


def rotary_tables(offset):
    half_dim = HEAD_DIM // 2
    inverse = jnp.exp(
        jnp.arange(half_dim, dtype=jnp.float32) * (-2.0 * math.log(10000.0) / HEAD_DIM)
    )
    angles = offset.astype(jnp.float32)[..., None] * inverse
    return (jnp.cos(angles), jnp.sin(angles))


def rotate(values, cosine, sine):
    half_dim = values.shape[-1] // 2
    front_half = values[..., :half_dim]
    back_half = values[..., half_dim:]
    cos_wide = cosine[..., None, :]
    sin_wide = sine[..., None, :]
    return jnp.concatenate(
        [
            front_half * cos_wide - back_half * sin_wide,
            back_half * cos_wide + front_half * sin_wide,
        ],
        axis=-1,
    )


def swiglu(gate_up):
    half_cols = gate_up.shape[-1] // 2
    return jax.nn.silu(gate_up[:, :half_cols]) * gate_up[:, half_cols:]


def adam_update(weight, first_moment, second_moment, gradient, factor, use_decay, rate):
    clipped = gradient * factor
    first_new = beta_one * first_moment + (1.0 - beta_one) * clipped
    second_new = beta_two * second_moment + (1.0 - beta_two) * clipped * clipped
    first_hat = first_new / (1.0 - beta_one**STEP)
    second_hat = second_new / (1.0 - beta_two**STEP)
    direction = first_hat / (jnp.sqrt(second_hat) + adam_eps) + use_decay * weight_decay * weight
    return (clipped, weight - rate * direction, first_new, second_new)


def contract_rows(left, right):
    return lax.dot_general(
        left, right, (((0,), (0,)), ((), ())), preferred_element_type=jnp.float32
    )


def contract_cols(left, right):
    return lax.dot_general(
        left, right, (((1,), (1,)), ((), ())), preferred_element_type=jnp.float32
    )


def per_device(
    tokens,
    cotangent,
    lengths,
    qkv_master,
    qkv_first,
    qkv_second,
    out_master,
    out_first,
    out_second,
    in_master,
    in_first,
    in_second,
    down_master,
    down_first,
    down_second,
    norm_gains,
    gain_first,
    gain_second,
):
    heads_local = HEADS // lax.axis_size("tensor")
    width_local = heads_local * HEAD_DIM
    ffn_local = FF // lax.axis_size("tensor")
    row_count = lengths.shape[0]
    all_rows = row_count * ROW
    score_scale = HEAD_DIM ** (-0.5)
    block_rows = min(512, ROW)
    block_count = ROW // block_rows
    w_qkv, w_out, w_in, w_down = (
        lax.all_gather(qkv_master.astype(jnp.bfloat16), "dp", axis=0, tiled=True),
        lax.all_gather(out_master.astype(jnp.bfloat16), "dp", axis=0, tiled=True),
        lax.all_gather(in_master.astype(jnp.bfloat16), "dp", axis=0, tiled=True),
        lax.all_gather(down_master.astype(jnp.bfloat16), "dp", axis=0, tiled=True),
    )
    w_qkv = w_qkv.reshape(D, 3 * width_local)
    w_in = w_in.reshape(D, 2 * ffn_local)
    segment, offset = row_layout(lengths)
    cosine, sine = rotary_tables(offset)
    gain_one = norm_gains[0]
    gain_two = norm_gains[1]
    inputs = tokens.astype(jnp.float32)
    normed = layer_norm(inputs, gain_one)
    gathered_one = lax.all_gather(normed.astype(jnp.bfloat16), "tensor", axis=0, tiled=True)
    projected = jnp.dot(gathered_one, w_qkv, preferred_element_type=jnp.float32)
    projected = projected.reshape(row_count, ROW, 3, heads_local, HEAD_DIM)
    queries = rotate(projected[:, :, 0], cosine, sine).astype(jnp.bfloat16)
    keys = rotate(projected[:, :, 1], cosine, sine).astype(jnp.bfloat16)
    values = projected[:, :, 2].astype(jnp.bfloat16)

    def score_block(query_block, key_row, segment_block, segment_row):
        scores = (
            jnp.einsum("qhd,khd->hqk", query_block, key_row, preferred_element_type=jnp.float32)
            * score_scale
        )
        allowed = segment_block[:, None] == segment_row[None, :]
        return jnp.where(allowed[None], scores, -1e30)

    def forward_row(pieces):
        query_row, key_row, value_row, segment_row = pieces

        def forward_block(block_parts):
            query_block, segment_block = block_parts
            masked = score_block(query_block, key_row, segment_block, segment_row)
            row_max = jnp.max(masked, axis=-1, keepdims=True)
            log_total = (
                jnp.log(jnp.sum(jnp.exp(masked - row_max), axis=-1, keepdims=True)) + row_max
            )
            weights = jnp.exp(masked - log_total).astype(jnp.bfloat16)
            mixed_heads = jnp.einsum(
                "hqk,khd->qhd", weights, value_row, preferred_element_type=jnp.float32
            )
            return (mixed_heads.astype(jnp.bfloat16), log_total)

        return lax.map(
            forward_block,
            (
                query_row.reshape(block_count, block_rows, heads_local, HEAD_DIM),
                segment_row.reshape(block_count, block_rows),
            ),
        )

    mixed_heads, log_totals = lax.map(forward_row, (queries, keys, values, segment))
    attended = mixed_heads.reshape(all_rows, width_local)
    middle = inputs + lax.psum_scatter(
        jnp.dot(attended, w_out, preferred_element_type=jnp.float32),
        "tensor",
        scatter_dimension=0,
        tiled=True,
    )
    normed_two = layer_norm(middle, gain_two)
    gathered_two = lax.all_gather(normed_two.astype(jnp.bfloat16), "tensor", axis=0, tiled=True)
    gate_up = jnp.dot(gathered_two, w_in, preferred_element_type=jnp.float32)
    hidden = swiglu(gate_up).astype(jnp.bfloat16)
    output = middle + lax.psum_scatter(
        jnp.dot(hidden, w_down, preferred_element_type=jnp.float32).astype(jnp.bfloat16),
        "tensor",
        scatter_dimension=0,
        tiled=True,
    ).astype(jnp.float32)
    layer_out = output.astype(jnp.bfloat16)
    upstream = cotangent.astype(jnp.float32)
    gathered_down = lax.all_gather(cotangent, "tensor", axis=0, tiled=True)
    grad_down = contract_rows(hidden, gathered_down)
    hidden_grad = contract_cols(gathered_down, w_down)
    gate_up_grad = jax.vjp(swiglu, gate_up)[1](hidden_grad)[0].astype(jnp.bfloat16)
    grad_in = contract_rows(gathered_two, gate_up_grad)
    normed_two_grad = lax.psum_scatter(
        contract_cols(gate_up_grad, w_in).astype(jnp.bfloat16),
        "tensor",
        scatter_dimension=0,
        tiled=True,
    ).astype(jnp.float32)
    middle_back, gain_two_grad = jax.vjp(layer_norm, middle, gain_two)[1](normed_two_grad)
    middle_grad = upstream + middle_back
    gathered_mid = lax.all_gather(middle_grad.astype(jnp.bfloat16), "tensor", axis=0, tiled=True)
    grad_out = contract_rows(attended, gathered_mid)
    attended_grad = contract_cols(gathered_mid, w_out).astype(jnp.bfloat16)
    attended_grad = attended_grad.reshape(row_count, ROW, heads_local, HEAD_DIM)

    def backward_row(pieces):
        query_row, key_row, value_row, segment_row, total_row, grad_row = pieces

        def backward_block(running, block_parts):
            key_acc, value_acc = running
            query_block, segment_block, total_block, grad_block = block_parts
            masked = score_block(query_block, key_row, segment_block, segment_row)
            probs_block = jnp.exp(masked - total_block)
            probs_low = probs_block.astype(jnp.bfloat16)
            prob_grad = jnp.einsum(
                "qhd,khd->hqk", grad_block, value_row, preferred_element_type=jnp.float32
            )
            row_inner = jnp.sum(probs_block * prob_grad, axis=-1, keepdims=True)
            score_grad = (probs_block * (prob_grad - row_inner)).astype(jnp.bfloat16)
            query_grad = (
                jnp.einsum("hqk,khd->qhd", score_grad, key_row, preferred_element_type=jnp.float32)
                * score_scale
            )
            key_acc = (
                key_acc
                + jnp.einsum(
                    "hqk,qhd->khd", score_grad, query_block, preferred_element_type=jnp.float32
                )
                * score_scale
            )
            value_acc = value_acc + jnp.einsum(
                "hqk,qhd->khd", probs_low, grad_block, preferred_element_type=jnp.float32
            )
            return ((key_acc, value_acc), query_grad)

        zeros_acc = jnp.zeros((ROW, heads_local, HEAD_DIM), jnp.float32)
        block_inputs = (
            query_row.reshape(block_count, block_rows, heads_local, HEAD_DIM),
            segment_row.reshape(block_count, block_rows),
            total_row,
            grad_row.reshape(block_count, block_rows, heads_local, HEAD_DIM),
        )
        (key_grad, value_grad), query_grad = lax.scan(
            backward_block, (zeros_acc, zeros_acc), block_inputs
        )
        return (query_grad.reshape(ROW, heads_local, HEAD_DIM), key_grad, value_grad)

    query_grad, key_grad, value_grad = lax.map(
        backward_row, (queries, keys, values, segment, log_totals, attended_grad)
    )
    rotate_back = jax.vjp(partial(rotate, cosine=cosine, sine=sine), projected[:, :, 0])[1]
    query_raw = rotate_back(query_grad)[0]
    key_raw = rotate_back(key_grad)[0]
    qkv_grad_low = (
        jnp.stack([query_raw, key_raw, value_grad], axis=2)
        .reshape(all_rows, 3 * width_local)
        .astype(jnp.bfloat16)
    )
    grad_qkv = contract_rows(gathered_one, qkv_grad_low)
    normed_grad = lax.psum_scatter(
        contract_cols(qkv_grad_low, w_qkv).astype(jnp.bfloat16),
        "tensor",
        scatter_dimension=0,
        tiled=True,
    ).astype(jnp.float32)
    input_back, gain_one_grad = jax.vjp(layer_norm, inputs, gain_one)[1](normed_grad)
    input_grad = middle_grad + input_back
    reduced_qkv, reduced_out, reduced_in, reduced_down = (
        lax.psum_scatter(
            grad_qkv.reshape(D, 3, width_local).astype(jnp.bfloat16),
            "dp",
            scatter_dimension=0,
            tiled=True,
        ).astype(jnp.float32),
        lax.psum_scatter(
            grad_out.astype(jnp.bfloat16), "dp", scatter_dimension=0, tiled=True
        ).astype(jnp.float32),
        lax.psum_scatter(
            grad_in.reshape(D, 2, ffn_local).astype(jnp.bfloat16),
            "dp",
            scatter_dimension=0,
            tiled=True,
        ).astype(jnp.float32),
        lax.psum_scatter(
            grad_down.astype(jnp.bfloat16), "dp", scatter_dimension=0, tiled=True
        ).astype(jnp.float32),
    )
    local_squares = (
        jnp.sum(reduced_qkv * reduced_qkv)
        + jnp.sum(reduced_out * reduced_out)
        + jnp.sum(reduced_in * reduced_in)
        + jnp.sum(reduced_down * reduced_down)
    )
    gain_part = jnp.stack([gain_one_grad, gain_two_grad])
    gain_total, weight_squares = lax.psum((gain_part, local_squares), ("dp", "tensor"))
    grad_norm = jnp.sqrt(weight_squares + jnp.sum(gain_total * gain_total))
    factor = max_norm / jnp.maximum(grad_norm, max_norm)
    qkv_res = adam_update(qkv_master, qkv_first, qkv_second, reduced_qkv, factor, 1.0, learn_rate)
    out_res = adam_update(out_master, out_first, out_second, reduced_out, factor, 1.0, learn_rate)
    in_res = adam_update(in_master, in_first, in_second, reduced_in, factor, 1.0, learn_rate)
    down_res = adam_update(
        down_master, down_first, down_second, reduced_down, factor, 1.0, learn_rate
    )
    gain_res = adam_update(norm_gains, gain_first, gain_second, gain_total, factor, 0.0, gain_rate)
    return (
        layer_out,
        input_grad,
        qkv_res[0],
        qkv_res[1],
        qkv_res[2],
        qkv_res[3],
        out_res[0],
        out_res[1],
        out_res[2],
        out_res[3],
        in_res[0],
        in_res[1],
        in_res[2],
        in_res[3],
        down_res[0],
        down_res[1],
        down_res[2],
        down_res[3],
        gain_res[0],
        gain_res[1],
        gain_res[2],
        gain_res[3],
        grad_norm,
    )


def solution(mesh):
    placed = (
        P(("dp", "tensor"), None),
        P(("dp", "tensor"), None),
        P("dp", None),
        P("dp", None, "tensor"),
        P("dp", None, "tensor"),
        P("dp", None, "tensor"),
        P(("tensor", "dp"), None),
        P(("tensor", "dp"), None),
        P(("tensor", "dp"), None),
        P("dp", None, "tensor"),
        P("dp", None, "tensor"),
        P("dp", None, "tensor"),
        P(("tensor", "dp"), None),
        P(("tensor", "dp"), None),
        P(("tensor", "dp"), None),
        P(),
        P(),
        P(),
    )
    return jax.shard_map(
        per_device,
        mesh=mesh,
        in_specs=placed,
        out_specs=(
            P(("dp", "tensor"), None),
            P(("dp", "tensor"), None),
            P("dp", None, "tensor"),
            P("dp", None, "tensor"),
            P("dp", None, "tensor"),
            P("dp", None, "tensor"),
            P(("tensor", "dp"), None),
            P(("tensor", "dp"), None),
            P(("tensor", "dp"), None),
            P(("tensor", "dp"), None),
            P("dp", None, "tensor"),
            P("dp", None, "tensor"),
            P("dp", None, "tensor"),
            P("dp", None, "tensor"),
            P(("tensor", "dp"), None),
            P(("tensor", "dp"), None),
            P(("tensor", "dp"), None),
            P(("tensor", "dp"), None),
            P(),
            P(),
            P(),
            P(),
            P(),
        ),
        check_vma=False,
    )
```

profile of v0, /device:TPU:0, one launch (start us, length us, event | category | flops | bytes accessed | tf_op | source)
XLA Modules:
  0.0 1104.4 jit_solution(1875028781626215786)
XLA Ops:
  16.8 36.3 %all_gather.26 = bf16[256,1024]{1,0:T(8,128)(2,1)} all-gather(bf16[32,1024]{1,0:T(8,128)(2,1)S(1)} %convert_element_type.159), channel_id=1, replica_groups=mesh['dp'=8,'tensor'=4] {'dp'}, dimensions={0}, use_global_device_ids=true | all-gather | bytes 589824 | tf_op jit(solution)/shard_map/all_gather | solution.py:120
  61.6 35.9 %all-gather.8.cloned.1.call-done = bf16[2048,1024]{1,0:T(8,128)(2,1)} async-done(((bf16[512,1024]{1,0:T(8,128)(2,1)}), bf16[2048,1024]{1,0:T(8,128)(2,1)}) %all-gather.8.cloned.1.call-update) | async-done | bytes 4194320 | tf_op jit(solution)/shard_map/all_gather | solution.py:132
  110.1 57.2 %while.47 = (s32[]{:T(128)}, bf16[4,512,4,64]{1,3,2,0:T(8,128)(2,1)}, f32[4,4,512,1]{2,1,3,0:T(4,128)}, s32[4,512]{1,0:T(4,128)S(1)}, s32[2048]{0:T(1024)S(1)}, ...) while((s32[]{:T(128)}, ...), condition=%wide.region_8.9_spmd, body=%wide.region_5.8_spmd.sunk | while | flops 1121056768 | bytes 57227380 | solution.py:163
  178.4 69.5 %reduce-scatter.8.cloned.1.call-done = f32[512,1024]{1,0:T(8,128)} async-done(((f32[2048,1024]{1,0:T(8,128)}), f32[512,1024]{1,0:T(8,128)}) %reduce-scatter.8.cloned.1.call-update) | async-done | bytes 2097168 | tf_op jit(solution)/shard_map/reduce_scatter | solution.py:173
  254.4 69.7 %all-gather.14.cloned.1.call-done = bf16[1024,2,1024]{2,1,0:T(2,128)(2,1)} async-done(((bf16[128,2,1024]{2,1,0:T(2,128)(2,1)}), bf16[1024,2,1024]{2,1,0:T(2,128)(2,1)}) %all-gather.14.cloned.1.call-update) | async-done | bytes 4194320 | tf_op jit(solution)/shard_map/all_gather | solution.py:121
  329.7 29.2 %all-gather.12.cloned.1.call-done = bf16[2048,1024]{1,0:T(8,128)(2,1)} async-done(((bf16[512,1024]{1,0:T(8,128)(2,1)}), bf16[2048,1024]{1,0:T(8,128)(2,1)}) %all-gather.12.cloned.1.call-update) | async-done | bytes 4194320 | tf_op jit(solution)/shard_map/all_gather | solution.py:180
  358.9 15.1 %fusion.96 = f32[2048,2048]{1,0:T(8,128)} fusion(bf16[2048,1024]{1,0:T(8,128)(2,1)} %all-gather.12.cloned.1.call-done, bf16[1024,2048]{1,0:T(8,128)(2,1)} %bitcast.176), kind=kOutput, calls=%fused_computation.180 | convolution fusion | flops 8589934592 | bytes 25165824 | tf_op jit(solution)/shard_map/dot_general | solution.py:181
  374.0 37.0 %all-gather.16.cloned.1.call-done = bf16[1024,1024]{1,0:T(8,128)(2,1)} async-done(((bf16[128,1024]{1,0:T(8,128)(2,1)}), bf16[1024,1024]{1,0:T(8,128)(2,1)}) %all-gather.16.cloned.1.call-update) | async-done | bytes 2097168 | tf_op jit(solution)/shard_map/all_gather | solution.py:122
  411.0 34.6 %all-gather.18.cloned.1.call-done = bf16[2048,1024]{1,0:T(8,128)(2,1)} async-done(((bf16[512,1024]{1,0:T(8,128)(2,1)}), bf16[2048,1024]{1,0:T(8,128)(2,1)}) %all-gather.18.cloned.1.call-update) | async-done | bytes 4194320 | tf_op jit(solution)/shard_map/all_gather | solution.py:191
  445.6 17.2 %fusion.73 = (f32[2048,1024]{1,0:T(8,128)}, f32[2048,1024]{1,0:T(8,128)}, bf16[2048,1024]{1,0:T(8,128)(2,1)}) fusion(f32[2048,2048]{1,0:T(8,128)} %fusion.96, bf16[2048,1024]{1,0:T(8,128)(2,1)} %all-gather.18.cloned.1.call-done, bf16[1024,1024]{1,0:T(8,128)(2,1)} %all-gather.16.cloned.1.call-done), kind=kOutput, calls=%fused_computation.124 | convolution fusion | flops 4324327424 | bytes 44040192 | tf_op jit(solution)/shard_map/dot_general | solution.py:85
  462.8 15.0 %convolution_convert_fusion.1 = bf16[2048,1024]{1,0:T(8,128)(2,1)} fusion(bf16[1024,2048]{1,0:T(8,128)(2,1)} %bitcast.177, f32[2048,1024]{1,0:T(8,128)} %get-tuple-element.338, f32[2048,1024]{1,0:T(8,128)} %get-tuple-element.337), kind=kOutput, calls=%fused_computation.65 | convolution fusion | flops 8600420352 | bytes 25165824 | tf_op jit(solution)/shard_map/dot_general | solution.py:85
  488.0 34.6 %reduce-scatter.12.cloned.1.call-done = bf16[512,1024]{1,0:T(8,128)(2,1)} async-done(((bf16[2048,1024]{1,0:T(8,128)(2,1)}), bf16[512,1024]{1,0:T(8,128)(2,1)}) %reduce-scatter.12.cloned.1.call-update) | async-done | bytes 1048592 | tf_op jit(solution)/shard_map/reduce_scatter | solution.py:196
  525.3 44.4 %reduce-scatter.10.cloned.1.call-done = bf16[512,1024]{1,0:T(8,128)(2,1)} async-done(((bf16[2048,1024]{1,0:T(8,128)(2,1)}), bf16[512,1024]{1,0:T(8,128)(2,1)}) %reduce-scatter.10.cloned.1.call-update) | async-done | bytes 1048592 | tf_op jit(solution)/shard_map/reduce_scatter | solution.py:183
  575.8 17.0 %convolution_convert_fusion = bf16[1024,2048]{1,0:T(8,128)(2,1)} fusion(bf16[2048,1024]{1,0:T(8,128)(2,1)} %all-gather.12.cloned.1.call-done, f32[2048,1024]{1,0:T(8,128)} %get-tuple-element.338, f32[2048,1024]{1,0:T(8,128)} %get-tuple-element.337), kind=kOutput, calls=%fused_computation.64 | convolution fusion | flops 8600420352 | bytes 25165824 | tf_op jit(solution)/shard_map/dot_general | solution.py:79
  620.5 230.1 %while.48 = (s32[]{:T(128)}, f32[2048,4,64]{0,2,1:T(8,128)}, f32[2048,4,64]{0,2,1:T(8,128)}, f32[4,512,4,64]{1,0,3,2:T(4,128)}, bf16[4,512,4,64]{1,3,2,0:T(8,128...) while((s32[]{:T(128)}, f32[2048,4,64]{0,2,1:T(8,128)}, ...), condition=%wide.region_18.19_spmd.clone, body=%wide.region_16.18_spmd.clone.sunk | while | flops 2751068160 | bytes 183179600 | solution.py:246
  632.8 11.5 %multiply_reduce_fusion.4 = (f32[4,512]{1,0:T(4,128)}, f32[4,512,2048]{2,1,0:T(8,128)}) fusion(f32[4,512,2048]{2,1,0:T(8,128)S(1)} %fusion.154, f32[4,512]{1,0:T(4,128)S(1)} %dynamic-slice_bitcast_fusion.2, pred[512,2048]{1,0:T(8,128)(4,1)} %copy-done.1, bf16[2048,4,64]{0,2,1:T(8,128)(2,1)} %get-tuple-element.552, ...), kind=kOutput, calls=%fused_computation.20.clone.1 | convolution fusion | flops 557840384 | bytes 35930116 | tf_op jit(solution)/shard_map/while/body/eval_jaxpr/while/body/eval_jaxpr/qhd,khd->hqk/dot_general | solution.py:218
  644.4 11.2 %multiply_convert_fusion.4 = bf16[4,512,2048]{2,1,0:T(8,128)(2,1)} fusion(f32[4,512,2048]{2,1,0:T(8,128)} %get-tuple-element.487, f32[4,512,2048]{2,1,0:T(8,128)S(1)} %fusion.154, f32[4,512]{1,0:T(4,128)} %get-tuple-element.488, f32[4,512]{1,0:T(4,128)S(1)} %dynamic-slice_bitcast_fusion.2, pred[512,2048]{1,0:T(8,128)(4,1)} %copy-done.1), kind=kLoop, calls=%fused_computation.19.clone.1 | loop fusion | flops 25165824 | bytes 43008000 | tf_op jit(solution)/shard_map/while/body/eval_jaxpr/while/body/eval_jaxpr/convert_element_type | solution.py:222
  689.9 11.5 %multiply_reduce_fusion.4 = (f32[4,512]{1,0:T(4,128)}, f32[4,512,2048]{2,1,0:T(8,128)}) fusion(f32[4,512,2048]{2,1,0:T(8,128)S(1)} %fusion.154, f32[4,512]{1,0:T(4,128)S(1)} %dynamic-slice_bitcast_fusion.2, pred[512,2048]{1,0:T(8,128)(4,1)} %copy-done.1, bf16[2048,4,64]{0,2,1:T(8,128)(2,1)} %get-tuple-element.552, ...), kind=kOutput, calls=%fused_computation.20.clone.1 | convolution fusion | flops 557840384 | bytes 35930116 | tf_op jit(solution)/shard_map/while/body/eval_jaxpr/while/body/eval_jaxpr/qhd,khd->hqk/dot_general | solution.py:218
  747.6 11.5 %multiply_reduce_fusion.4 = (f32[4,512]{1,0:T(4,128)}, f32[4,512,2048]{2,1,0:T(8,128)}) fusion(f32[4,512,2048]{2,1,0:T(8,128)S(1)} %fusion.154, f32[4,512]{1,0:T(4,128)S(1)} %dynamic-slice_bitcast_fusion.2, pred[512,2048]{1,0:T(8,128)(4,1)} %copy-done.1, bf16[2048,4,64]{0,2,1:T(8,128)(2,1)} %get-tuple-element.552, ...), kind=kOutput, calls=%fused_computation.20.clone.1 | convolution fusion | flops 557840384 | bytes 35930116 | tf_op jit(solution)/shard_map/while/body/eval_jaxpr/while/body/eval_jaxpr/qhd,khd->hqk/dot_general | solution.py:218
  805.3 11.5 %multiply_reduce_fusion.4 = (f32[4,512]{1,0:T(4,128)}, f32[4,512,2048]{2,1,0:T(8,128)}) fusion(f32[4,512,2048]{2,1,0:T(8,128)S(1)} %fusion.154, f32[4,512]{1,0:T(4,128)S(1)} %dynamic-slice_bitcast_fusion.2, pred[512,2048]{1,0:T(8,128)(4,1)} %copy-done.1, bf16[2048,4,64]{0,2,1:T(8,128)(2,1)} %get-tuple-element.552, ...), kind=kOutput, calls=%fused_computation.20.clone.1 | convolution fusion | flops 557840384 | bytes 35930116 | tf_op jit(solution)/shard_map/while/body/eval_jaxpr/while/body/eval_jaxpr/qhd,khd->hqk/dot_general | solution.py:218
  883.5 37.6 %reduce-scatter.18.cloned.1.call-done = bf16[32,1024]{1,0:T(8,128)(2,1)} async-done(((bf16[256,1024]{1,0:T(8,128)(2,1)}), bf16[32,1024]{1,0:T(8,128)(2,1)}) %reduce-scatter.18.cloned.1.call-update) | async-done | bytes 65552 | tf_op jit(solution)/shard_map/reduce_scatter | solution.py:278
  922.6 66.9 %reduce-scatter.16.cloned.1.call-done = bf16[128,3,256]{2,0,1:T(8,128)(2,1)} async-done(((bf16[1024,3,256]{2,0,1:T(8,128)(2,1)}), bf16[128,3,256]{2,0,1:T(8,128)(2,1)}) %reduce-scatter.16.cloned.1.call-update) | async-done | bytes 196624 | tf_op jit(solution)/shard_map/reduce_scatter | solution.py:272
  993.7 41.8 %reduce-scatter.14.cloned.1.call-done = bf16[512,1024]{1,0:T(8,128)(2,1)} async-done(((bf16[2048,1024]{1,0:T(8,128)(2,1)}), bf16[512,1024]{1,0:T(8,128)(2,1)}) %reduce-scatter.14.cloned.1.call-update) | async-done | bytes 1048592 | tf_op jit(solution)/shard_map/reduce_scatter | solution.py:263
  1039.7 39.7 %all-reduce.7 = (f32[]{:T(128)}, f32[2,1024]{1,0:T(2,128)S(1)}) all-reduce(f32[]{:T(128)S(6)} %add.210, f32[2,1024]{1,0:T(2,128)S(1)} %pad_maximum_fusion.1), channel_id=1, replica_groups=mesh['dp'=8,'tensor'=4] {'dp','tensor'}, use_global_device_ids=true, to_apply=%region_30.31 | all-reduce | flops 2049 | bytes 16392 | tf_op jit(solution)/shard_map/psum | solution.py:298
  (321 shorter events, 384.1 us)
Async XLA Ops:
  7.2 54.4 %all-gather.10.cloned.1.call-start = ((), (), s32[]{:S(2)}) async-start(), calls=%async_computation.8 | async-start | bytes 1769472 | tf_op jit(solution)/shard_map/all_gather | solution.py:119
  9.1 88.4 %all-gather.8.cloned.1.call-start = ((), (), s32[]{:S(2)}) async-start(), calls=%async_computation.7 | async-start | bytes 5242880 | tf_op jit(solution)/shard_map/all_gather | solution.py:132
  16.3 231.6 %reduce-scatter.8.cloned.1.call-start = ((), (), s32[]{:S(2)}) async-start(), calls=%async_computation.9 | async-start | bytes 10485760 | tf_op jit(solution)/shard_map/reduce_scatter | solution.py:173
  176.0 148.1 %all-gather.14.cloned.1.call-start = ((), (), s32[]{:S(2)}) async-start(), calls=%async_computation.11 | async-start | bytes 4718592 | tf_op jit(solution)/shard_map/all_gather | solution.py:121
  178.4 180.5 %all-gather.12.cloned.1.call-start = ((), (), s32[]{:S(2)}) async-start(), calls=%async_computation.10 | async-start | bytes 5242880 | tf_op jit(solution)/shard_map/all_gather | solution.py:180
  251.7 159.3 %all-gather.16.cloned.1.call-start = ((), (), s32[]{:S(2)}) async-start(), calls=%async_computation.12 | async-start | bytes 2359296 | tf_op jit(solution)/shard_map/all_gather | solution.py:122
  253.6 192.1 %all-gather.18.cloned.1.call-start = ((), (), s32[]{:S(2)}) async-start(), calls=%async_computation.14 | async-start | bytes 5242880 | tf_op jit(solution)/shard_map/all_gather | solution.py:191
  254.3 268.3 %reduce-scatter.12.cloned.1.call-start = ((), (), s32[]{:S(2)}) async-start(), calls=%async_computation.15 | async-start | bytes 5242880 | tf_op jit(solution)/shard_map/reduce_scatter | solution.py:196
  477.9 91.8 %reduce-scatter.10.cloned.1.call-start = ((), (), s32[]{:S(2)}) async-start(), calls=%async_computation.13 | async-start | bytes 5242880 | tf_op jit(solution)/shard_map/reduce_scatter | solution.py:183
  488.0 122.4 %all-gather.20.cloned.1.call-start = ((), (), s32[]{:S(2)}) async-start(), calls=%async_computation.16 | async-start | bytes 5242880 | tf_op jit(solution)/shard_map/all_gather | solution.py:204
  575.7 303.3 %all-reduce.10.cloned.1.call-start = ((), (), s32[]{:S(2)}) async-start(), calls=%async_computation.21 | async-start | bytes 8388608
  600.7 281.1 %reduce-scatter.20.cloned.1.call-start = ((), (), s32[]{:S(2)}) async-start(), calls=%async_computation.20 | async-start | bytes 2359296 | tf_op jit(solution)/shard_map/reduce_scatter | solution.py:287
  610.3 310.8 %reduce-scatter.18.cloned.1.call-start = ((), (), s32[]{:S(2)}) async-start(), calls=%async_computation.19 | async-start | bytes 589824 | tf_op jit(solution)/shard_map/reduce_scatter | solution.py:278
  858.7 130.7 %reduce-scatter.16.cloned.1.call-start = ((), (), s32[]{:S(2)}) async-start(), calls=%async_computation.18 | async-start | bytes 1769472 | tf_op jit(solution)/shard_map/reduce_scatter | solution.py:272
  870.1 165.4 %reduce-scatter.14.cloned.1.call-start = ((), (), s32[]{:S(2)}) async-start(), calls=%async_computation.17 | async-start | bytes 5242880 | tf_op jit(solution)/shard_map/reduce_scatter | solution.py:263
  877.2 158.3 %copy-start.41 = (f32[512]{0:T(512)S(1)}, f32[512]{0:T(512)}, u32[]{:S(2)}) copy-start(f32[512]{0:T(512)} %copy-done.40) | copy-start | bytes 6148
  877.2 160.1 %copy-start.48 = (f32[512]{0:T(512)S(1)}, f32[512]{0:T(512)}, u32[]{:S(2)}) copy-start(f32[512]{0:T(512)} %copy-done.47) | copy-start | bytes 6148
  877.2 160.1 %copy-start.44 = (f32[512]{0:T(512)S(1)}, f32[512]{0:T(512)}, u32[]{:S(2)}) copy-start(f32[512]{0:T(512)} %copy-done.43) | copy-start | bytes 6148
  877.2 162.5 %copy-start.49 = (f32[1024]{0:T(1024)S(1)}, f32[1024]{0:T(1024)}, u32[]{:S(2)}) copy-start(f32[1024]{0:T(1024)} %get-tuple-element.261) | copy-start | bytes 12292
  877.2 204.3 %copy-start.42 = (f32[2,1024]{1,0:T(2,128)S(1)}, f32[2,1024]{1,0:T(2,128)}, u32[]{:S(2)}) copy-start(f32[2,1024]{1,0:T(2,128)} %param.37) | copy-start | bytes 24580
  877.2 204.3 %copy-start.50 = (f32[2,1024]{1,0:T(2,128)S(1)}, f32[2,1024]{1,0:T(2,128)}, u32[]{:S(2)}) copy-start(f32[2,1024]{1,0:T(2,128)} %param.38) | copy-start | bytes 24580
  877.2 204.3 %copy-start.51 = (f32[2,1024]{1,0:T(2,128)S(1)}, f32[2,1024]{1,0:T(2,128)}, u32[]{:S(2)}) copy-start(f32[2,1024]{1,0:T(2,128)} %param.39) | copy-start | bytes 24580
  877.3 204.9 %copy-start.7 = (f32[512,1024]{1,0:T(8,128)S(1)}, f32[512,1024]{1,0:T(8,128)}, u32[]{:S(2)}) copy-start(f32[512,1024]{1,0:T(8,128)} %copy-done.6) | copy-start | bytes 6291460
  877.3 204.9 %copy-start.46 = (f32[512]{0:T(512)S(1)}, f32[512]{0:T(512)}, u32[]{:S(2)}) copy-start(f32[512]{0:T(512)} %copy-done.45) | copy-start | bytes 6148
  (65 other events, 810.9 us)
Sparse Core Ops, SparseCore 0:
  10.7 50.9 all-gather.9
  63.8 33.7 all-gather.7
  176.1 71.7 reduce-scatter.7
  250.6 73.3 all-gather.13
  326.1 32.7 all-gather.11
  361.7 49.2 all-gather.15
  412.6 32.9 all-gather.17
  478.0 44.5 reduce-scatter.11
  525.1 44.5 reduce-scatter.9
  575.9 34.4 all-gather.19
  614.5 156.3 all-reduce.9
  774.7 66.9 reduce-scatter.19
  858.9 62.1 reduce-scatter.17
  925.0 64.4 reduce-scatter.15
  992.0 43.4 reduce-scatter.13
where the time goes:
time: 1110 us; the launch traced here: 1100 us
  waiting for transfers between devices  510 us (46%)
  matrix products  283 us (25%)
  other arithmetic  125 us (11%)
  local copies, waits for them, and re-layouts  88.5 us (8%)
  blocking collectives  76 us (7%)
  between operations  20.7 us (2%)
    all_gather x1, waiting for transfers between devices, per_device(): lax.all_gather(in_master.astype(jnp.bfloat16), 'dp', axis=0, tiled=True)  69.7 us
    reduce_scatter x1, waiting for transfers between devices, per_device(): lax.psum_scatter(jnp.dot(attended, w_out, preferred_element_type=jnp.floa...  69.5 us
    reduce_scatter x1, waiting for transfers between devices, per_device(): lax.psum_scatter(grad_qkv.reshape(D, 3, width_local).astype(jnp.bfloat16)...  66.9 us
    dynamic_update_slice x8, local copies, waits for them, and re-layouts, backward_row(): lax.scan(backward_block, (zeros_acc, zeros_acc), block_inputs)  46.6 us
    dot_general x4, matrix products, backward_block(): jnp.einsum('qhd,khd->hqk', grad_block, value_row, preferred_element_type=...  46.1 us
    reduce_scatter x1, waiting for transfers between devices, per_device(): lax.psum_scatter(jnp.dot(hidden, w_down, preferred_element_type=jnp.float...  44.4 us
    convert_element_type x4, other arithmetic, backward_block(): score_grad = (probs_block * (prob_grad - row_inner)).astype(jnp.bfloat16)  44.2 us
    dot_general x4, matrix products, contract_cols(): lax.dot_general(left, right, (((1,), (1,)), ((), ())), preferred_element_...  43.7 us
  transfers between devices with their start and end apart: 15, of which 13 were waited for; matrix products, arithmetic and copies ran while one was open for 32% of the time, Pallas kernels for 0%

commit v1 on v0

--- a/solution.py
+++ b/solution.py
@@ -19,6 +19,28 @@
 weight_decay = 0.1
 adam_eps = 1e-08
 max_norm = 1.0
+
+
+def in_order(blocks, dim):
+    blocks = jnp.moveaxis(blocks, 0, dim)
+    shape = blocks.shape
+    return blocks.reshape(*shape[:dim], shape[dim] * shape[dim + 1], *shape[dim + 2 :])
+
+
+def doubled(shard, axis):
+    size = lax.axis_size(axis)
+    blocks = shard[None]
+    for level in range(size.bit_length() - 1):
+        bit = 1 << level
+        partner_block = lax.ppermute(blocks, axis, [(i, i ^ bit) for i in range(size)])
+        both = jnp.stack([blocks, partner_block])
+        upper = lax.axis_index(axis) >> level & 1
+        blocks = jnp.where(upper == 0, both, both[::-1]).reshape(-1, *shard.shape)
+    return blocks
+
+
+def collect(value, axis, dim):
+    return in_order(doubled(value, axis), dim)
 
 
 def layer_norm(values, gain):
@@ -129,7 +151,7 @@
     gain_two = norm_gains[1]
     inputs = tokens.astype(jnp.float32)
     normed = layer_norm(inputs, gain_one)
-    gathered_one = lax.all_gather(normed.astype(jnp.bfloat16), "tensor", axis=0, tiled=True)
+    gathered_one = collect(normed.astype(jnp.bfloat16), "tensor", 0)
     projected = jnp.dot(gathered_one, w_qkv, preferred_element_type=jnp.float32)
     projected = projected.reshape(row_count, ROW, 3, heads_local, HEAD_DIM)
     queries = rotate(projected[:, :, 0], cosine, sine).astype(jnp.bfloat16)

time: 1110 us -> 1090 us (0.982)
  waiting for transfers between devices: 510 us -> 480 us
    all_gather x1 -> x0, waiting for transfers between devices: 35.9 us -> none  [per_device(): lax.all_gather(normed.astype(jnp.bfloat16), 'tensor', axis=0, tiled=True)]
    ppermute x0 -> x2, waiting for transfers between devices: none -> 11.9 us  [doubled(): lax.ppermute(blocks, axis, [(i, i ^ bit) for i in range(size)])]
  transfers between devices with their start and end apart: 15 -> 16, of which waited for: 13 -> 13; matrix products, arithmetic and copies ran while one was open for 32% -> 33% of each run, Pallas kernels for 0% -> 0%
where the time goes in v1:
time: 1090 us; the launch traced here: 1080 us
  waiting for transfers between devices  480 us (44%)
  matrix products  283 us (26%)
  other arithmetic  132 us (12%)
  local copies, waits for them, and re-layouts  86.9 us (8%)
  blocking collectives  74 us (7%)
  between operations  20.7 us (2%)
    reduce_scatter x1, waiting for transfers between devices, per_device(): lax.psum_scatter(jnp.dot(attended, w_out, preferred_element_type=jnp.floa...  70.9 us
    all_gather x1, waiting for transfers between devices, per_device(): lax.all_gather(in_master.astype(jnp.bfloat16), 'dp', axis=0, tiled=True)  70 us
    reduce_scatter x1, waiting for transfers between devices, per_device(): lax.psum_scatter(grad_qkv.reshape(D, 3, width_local).astype(jnp.bfloat16)...  67.1 us
    dynamic_update_slice x8, local copies, waits for them, and re-layouts, backward_row(): lax.scan(backward_block, (zeros_acc, zeros_acc), block_inputs)  46.6 us
    dot_general x4, matrix products, backward_block(): jnp.einsum('qhd,khd->hqk', grad_block, value_row, preferred_element_type=...  46.1 us
    reduce_scatter x1, waiting for transfers between devices, per_device(): lax.psum_scatter(jnp.dot(hidden, w_down, preferred_element_type=jnp.float...  44.4 us
    convert_element_type x4, other arithmetic, backward_block(): score_grad = (probs_block * (prob_grad - row_inner)).astype(jnp.bfloat16)  44.3 us
    dot_general x4, matrix products, contract_cols(): lax.dot_general(left, right, (((1,), (1,)), ((), ())), preferred_element_...  43.8 us
  transfers between devices with their start and end apart: 16, of which 13 were waited for; matrix products, arithmetic and copies ran while one was open for 33% of the time, Pallas kernels for 0%

profile of v1, /device:TPU:0, one launch (start us, length us, event | category | flops | bytes accessed | tf_op | source)
XLA Modules:
  0.0 1080.9 jit_solution(5650951755416345517)
XLA Ops:
  22.2 34.3 %all_gather.22 = bf16[256,1024]{1,0:T(8,128)(2,1)} all-gather(bf16[32,1024]{1,0:T(8,128)(2,1)S(1)} %convert_element_type.159), channel_id=1, replica_groups=mesh['dp'=8,'tensor'=4] {'dp'}, dimensions={0}, use_global_device_ids=true | all-gather | bytes 589824 | tf_op jit(solution)/shard_map/all_gather | solution.py:142
  85.0 57.2 %while.47 = (s32[]{:T(128)}, bf16[4,512,4,64]{1,3,2,0:T(8,128)(2,1)}, f32[4,4,512,1]{2,1,3,0:T(4,128)}, s32[4,512]{1,0:T(4,128)S(1)}, s32[2048]{0:T(1024)S(1)}, ...) while((s32[]{:T(128)}, ...), condition=%wide.region_8.9_spmd, body=%wide.region_5.8_spmd.sunk | while | flops 1121056768 | bytes 57227380 | solution.py:185
  153.3 70.9 %reduce-scatter.8.cloned.1.call-done = f32[512,1024]{1,0:T(8,128)} async-done(((f32[2048,1024]{1,0:T(8,128)}), f32[512,1024]{1,0:T(8,128)}) %reduce-scatter.8.cloned.1.call-update) | async-done | bytes 2097168 | tf_op jit(solution)/shard_map/reduce_scatter | solution.py:195
  230.6 70.0 %all-gather.11.cloned.1.call-done = bf16[1024,2,1024]{2,1,0:T(2,128)(2,1)} async-done(((bf16[128,2,1024]{2,1,0:T(2,128)(2,1)}), bf16[1024,2,1024]{2,1,0:T(2,128)(2,1)}) %all-gather.11.cloned.1.call-update) | async-done | bytes 4194320 | tf_op jit(solution)/shard_map/all_gather | solution.py:143
  306.2 29.2 %all-gather.9.cloned.1.call-done = bf16[2048,1024]{1,0:T(8,128)(2,1)} async-done(((bf16[512,1024]{1,0:T(8,128)(2,1)}), bf16[2048,1024]{1,0:T(8,128)(2,1)}) %all-gather.9.cloned.1.call-update) | async-done | bytes 4194320 | tf_op jit(solution)/shard_map/all_gather | solution.py:202
  335.4 15.1 %fusion.90 = f32[2048,2048]{1,0:T(8,128)} fusion(bf16[2048,1024]{1,0:T(8,128)(2,1)} %all-gather.9.cloned.1.call-done, bf16[1024,2048]{1,0:T(8,128)(2,1)} %bitcast.185), kind=kOutput, calls=%fused_computation.184 | convolution fusion | flops 8589934592 | bytes 25165824 | tf_op jit(solution)/shard_map/dot_general | solution.py:203
  350.5 37.0 %all-gather.13.cloned.1.call-done = bf16[1024,1024]{1,0:T(8,128)(2,1)} async-done(((bf16[128,1024]{1,0:T(8,128)(2,1)}), bf16[1024,1024]{1,0:T(8,128)(2,1)}) %all-gather.13.cloned.1.call-update) | async-done | bytes 2097168 | tf_op jit(solution)/shard_map/all_gather | solution.py:144
  387.5 34.5 %all-gather.15.cloned.1.call-done = bf16[2048,1024]{1,0:T(8,128)(2,1)} async-done(((bf16[512,1024]{1,0:T(8,128)(2,1)}), bf16[2048,1024]{1,0:T(8,128)(2,1)}) %all-gather.15.cloned.1.call-update) | async-done | bytes 4194320 | tf_op jit(solution)/shard_map/all_gather | solution.py:213
  422.0 17.2 %fusion.65 = (f32[2048,1024]{1,0:T(8,128)}, f32[2048,1024]{1,0:T(8,128)}, bf16[2048,1024]{1,0:T(8,128)(2,1)}) fusion(f32[2048,2048]{1,0:T(8,128)} %fusion.90, bf16[2048,1024]{1,0:T(8,128)(2,1)} %all-gather.15.cloned.1.call-done, bf16[1024,1024]{1,0:T(8,128)(2,1)} %all-gather.13.cloned.1.call-done), kind=kOutput, calls=%fused_computation.126 | convolution fusion | flops 4324327424 | bytes 44040192 | tf_op jit(solution)/shard_map/dot_general | solution.py:107
  439.2 15.1 %convolution_convert_fusion.1 = bf16[2048,1024]{1,0:T(8,128)(2,1)} fusion(bf16[1024,2048]{1,0:T(8,128)(2,1)} %bitcast.186, f32[2048,1024]{1,0:T(8,128)} %get-tuple-element.338, f32[2048,1024]{1,0:T(8,128)} %get-tuple-element.337), kind=kOutput, calls=%fused_computation.62 | convolution fusion | flops 8600420352 | bytes 25165824 | tf_op jit(solution)/shard_map/dot_general | solution.py:107
  464.4 34.6 %reduce-scatter.12.cloned.1.call-done = bf16[512,1024]{1,0:T(8,128)(2,1)} async-done(((bf16[2048,1024]{1,0:T(8,128)(2,1)}), bf16[512,1024]{1,0:T(8,128)(2,1)}) %reduce-scatter.12.cloned.1.call-update) | async-done | bytes 1048592 | tf_op jit(solution)/shard_map/reduce_scatter | solution.py:218
  501.7 44.4 %reduce-scatter.10.cloned.1.call-done = bf16[512,1024]{1,0:T(8,128)(2,1)} async-done(((bf16[2048,1024]{1,0:T(8,128)(2,1)}), bf16[512,1024]{1,0:T(8,128)(2,1)}) %reduce-scatter.10.cloned.1.call-update) | async-done | bytes 1048592 | tf_op jit(solution)/shard_map/reduce_scatter | solution.py:205
  552.1 17.0 %convolution_convert_fusion = bf16[1024,2048]{1,0:T(8,128)(2,1)} fusion(bf16[2048,1024]{1,0:T(8,128)(2,1)} %all-gather.9.cloned.1.call-done, f32[2048,1024]{1,0:T(8,128)} %get-tuple-element.338, f32[2048,1024]{1,0:T(8,128)} %get-tuple-element.337), kind=kOutput, calls=%fused_computation.61 | convolution fusion | flops 8600420352 | bytes 25165824 | tf_op jit(solution)/shard_map/dot_general | solution.py:101
  596.9 230.1 %while.48 = (s32[]{:T(128)}, f32[2048,4,64]{0,2,1:T(8,128)}, f32[2048,4,64]{0,2,1:T(8,128)}, f32[4,512,4,64]{1,0,3,2:T(4,128)}, bf16[4,512,4,64]{1,3,2,0:T(8,128...) while((s32[]{:T(128)}, f32[2048,4,64]{0,2,1:T(8,128)}, ...), condition=%wide.region_18.19_spmd.clone, body=%wide.region_16.18_spmd.clone.sunk | while | flops 2751068160 | bytes 183179600 | solution.py:268
  609.2 11.5 %multiply_reduce_fusion.4 = (f32[4,512]{1,0:T(4,128)}, f32[4,512,2048]{2,1,0:T(8,128)}) fusion(f32[4,512,2048]{2,1,0:T(8,128)S(1)} %fusion.150, f32[4,512]{1,0:T(4,128)S(1)} %dynamic-slice_bitcast_fusion.2, pred[512,2048]{1,0:T(8,128)(4,1)} %copy-done.1, bf16[2048,4,64]{0,2,1:T(8,128)(2,1)} %get-tuple-element.556, ...), kind=kOutput, calls=%fused_computation.20.clone.1 | convolution fusion | flops 557840384 | bytes 35930116 | tf_op jit(solution)/shard_map/while/body/eval_jaxpr/while/body/eval_jaxpr/qhd,khd->hqk/dot_general | solution.py:240
  620.7 11.1 %multiply_convert_fusion.4 = bf16[4,512,2048]{2,1,0:T(8,128)(2,1)} fusion(f32[4,512,2048]{2,1,0:T(8,128)} %get-tuple-element.491, f32[4,512,2048]{2,1,0:T(8,128)S(1)} %fusion.150, f32[4,512]{1,0:T(4,128)} %get-tuple-element.492, f32[4,512]{1,0:T(4,128)S(1)} %dynamic-slice_bitcast_fusion.2, pred[512,2048]{1,0:T(8,128)(4,1)} %copy-done.1), kind=kLoop, calls=%fused_computation.19.clone.1 | loop fusion | flops 25165824 | bytes 43008000 | tf_op jit(solution)/shard_map/while/body/eval_jaxpr/while/body/eval_jaxpr/convert_element_type | solution.py:244
  666.3 11.5 %multiply_reduce_fusion.4 = (f32[4,512]{1,0:T(4,128)}, f32[4,512,2048]{2,1,0:T(8,128)}) fusion(f32[4,512,2048]{2,1,0:T(8,128)S(1)} %fusion.150, f32[4,512]{1,0:T(4,128)S(1)} %dynamic-slice_bitcast_fusion.2, pred[512,2048]{1,0:T(8,128)(4,1)} %copy-done.1, bf16[2048,4,64]{0,2,1:T(8,128)(2,1)} %get-tuple-element.556, ...), kind=kOutput, calls=%fused_computation.20.clone.1 | convolution fusion | flops 557840384 | bytes 35930116 | tf_op jit(solution)/shard_map/while/body/eval_jaxpr/while/body/eval_jaxpr/qhd,khd->hqk/dot_general | solution.py:240
  700.3 11.1 %dynamic_update_slice.33 = f32[4,512,4,64]{1,0,3,2:T(4,128)} dynamic-update-slice(f32[4,512,4,64]{1,0,3,2:T(4,128)} %get-tuple-element.536, f32[1,512,4,64]{1,0,3,2:T(1,128)S(1)} %copy.107, s32[]{:T(128)S(6)} %copy.125, s32[]{:T(128)} %constant.73.clone.1..sunk, s32[]{:T(128)} %constant.73.clone.1..sunk, s32[]{:T(128)} %constant.73.clone.1..sunk) | dynamic-update-slice | bytes 1048580 | tf_op jit(solution)/shard_map/while/body/eval_jaxpr/while/body/jit(dynamic_update_index_in_dim)/dynamic_update_slice | solution.py:268
  724.0 11.5 %multiply_reduce_fusion.4 = (f32[4,512]{1,0:T(4,128)}, f32[4,512,2048]{2,1,0:T(8,128)}) fusion(f32[4,512,2048]{2,1,0:T(8,128)S(1)} %fusion.150, f32[4,512]{1,0:T(4,128)S(1)} %dynamic-slice_bitcast_fusion.2, pred[512,2048]{1,0:T(8,128)(4,1)} %copy-done.1, bf16[2048,4,64]{0,2,1:T(8,128)(2,1)} %get-tuple-element.556, ...), kind=kOutput, calls=%fused_computation.20.clone.1 | convolution fusion | flops 557840384 | bytes 35930116 | tf_op jit(solution)/shard_map/while/body/eval_jaxpr/while/body/eval_jaxpr/qhd,khd->hqk/dot_general | solution.py:240
  781.7 11.5 %multiply_reduce_fusion.4 = (f32[4,512]{1,0:T(4,128)}, f32[4,512,2048]{2,1,0:T(8,128)}) fusion(f32[4,512,2048]{2,1,0:T(8,128)S(1)} %fusion.150, f32[4,512]{1,0:T(4,128)S(1)} %dynamic-slice_bitcast_fusion.2, pred[512,2048]{1,0:T(8,128)(4,1)} %copy-done.1, bf16[2048,4,64]{0,2,1:T(8,128)(2,1)} %get-tuple-element.556, ...), kind=kOutput, calls=%fused_computation.20.clone.1 | convolution fusion | flops 557840384 | bytes 35930116 | tf_op jit(solution)/shard_map/while/body/eval_jaxpr/while/body/eval_jaxpr/qhd,khd->hqk/dot_general | solution.py:240
  860.0 37.5 %reduce-scatter.18.cloned.1.call-done = bf16[32,1024]{1,0:T(8,128)(2,1)} async-done(((bf16[256,1024]{1,0:T(8,128)(2,1)}), bf16[32,1024]{1,0:T(8,128)(2,1)}) %reduce-scatter.18.cloned.1.call-update) | async-done | bytes 65552 | tf_op jit(solution)/shard_map/reduce_scatter | solution.py:300
  898.9 67.1 %reduce-scatter.16.cloned.1.call-done = bf16[128,3,256]{2,0,1:T(8,128)(2,1)} async-done(((bf16[1024,3,256]{2,0,1:T(8,128)(2,1)}), bf16[128,3,256]{2,0,1:T(8,128)(2,1)}) %reduce-scatter.16.cloned.1.call-update) | async-done | bytes 196624 | tf_op jit(solution)/shard_map/reduce_scatter | solution.py:294
  970.2 41.8 %reduce-scatter.14.cloned.1.call-done = bf16[512,1024]{1,0:T(8,128)(2,1)} async-done(((bf16[2048,1024]{1,0:T(8,128)(2,1)}), bf16[512,1024]{1,0:T(8,128)(2,1)}) %reduce-scatter.14.cloned.1.call-update) | async-done | bytes 1048592 | tf_op jit(solution)/shard_map/reduce_scatter | solution.py:285
  1016.2 39.7 %all-reduce.7 = (f32[]{:T(128)}, f32[2,1024]{1,0:T(2,128)S(1)}) all-reduce(f32[]{:T(128)S(6)} %add.210, f32[2,1024]{1,0:T(2,128)S(1)} %pad_maximum_fusion.3), channel_id=1, replica_groups=mesh['dp'=8,'tensor'=4] {'dp','tensor'}, use_global_device_ids=true, to_apply=%region_30.31 | all-reduce | flops 2049 | bytes 16392 | tf_op jit(solution)/shard_map/psum | solution.py:320
  (328 shorter events, 385.7 us)
Async XLA Ops:
  7.2 65.2 %all-gather.7.cloned.1.call-start = ((), (), s32[]{:S(2)}) async-start(), calls=%async_computation.7 | async-start | bytes 1769472 | tf_op jit(solution)/shard_map/all_gather | solution.py:141
  12.8 2.8 collective-permute-start
  18.0 49.1 %collective-permute-start.1 = (bf16[2,512,1024]{2,1,0:T(8,128)(2,1)}, bf16[2,512,1024]{2,1,0:T(8,128)(2,1)}, u32[]{:S(2)}, u32[]{:S(2)}) collective-permute-start(bf16[2,512,1024]{2,1,0:T(8,128)(2,1)} %get-tuple-element.352), channel_id=1, source_target_pairs={{0,2},{1,3},{2,0},{3,1},{4,6},{5,7},{6,4},{7,5},{8,10},{9,11},{10,... | collective-permute-start | bytes 6291464 | tf_op jit(solution)/shard_map/ppermute | solution.py:35
  21.7 202.5 %reduce-scatter.8.cloned.1.call-start = ((), (), s32[]{:S(2)}) async-start(), calls=%async_computation.8 | async-start | bytes 10485760 | tf_op jit(solution)/shard_map/reduce_scatter | solution.py:195
  150.9 149.7 %all-gather.11.cloned.1.call-start = ((), (), s32[]{:S(2)}) async-start(), calls=%async_computation.10 | async-start | bytes 4718592 | tf_op jit(solution)/shard_map/all_gather | solution.py:143
  153.3 182.2 %all-gather.9.cloned.1.call-start = ((), (), s32[]{:S(2)}) async-start(), calls=%async_computation.9 | async-start | bytes 5242880 | tf_op jit(solution)/shard_map/all_gather | solution.py:202
  228.1 159.4 %all-gather.13.cloned.1.call-start = ((), (), s32[]{:S(2)}) async-start(), calls=%async_computation.11 | async-start | bytes 2359296 | tf_op jit(solution)/shard_map/all_gather | solution.py:144
  229.9 192.1 %all-gather.15.cloned.1.call-start = ((), (), s32[]{:S(2)}) async-start(), calls=%async_computation.13 | async-start | bytes 5242880 | tf_op jit(solution)/shard_map/all_gather | solution.py:213
  230.5 268.5 %reduce-scatter.12.cloned.1.call-start = ((), (), s32[]{:S(2)}) async-start(), calls=%async_computation.14 | async-start | bytes 5242880 | tf_op jit(solution)/shard_map/reduce_scatter | solution.py:218
  454.3 91.7 %reduce-scatter.10.cloned.1.call-start = ((), (), s32[]{:S(2)}) async-start(), calls=%async_computation.12 | async-start | bytes 5242880 | tf_op jit(solution)/shard_map/reduce_scatter | solution.py:205
  464.4 122.4 %all-gather.17.cloned.1.call-start = ((), (), s32[]{:S(2)}) async-start(), calls=%async_computation.15 | async-start | bytes 5242880 | tf_op jit(solution)/shard_map/all_gather | solution.py:226
  552.1 303.4 %all-reduce.10.cloned.1.call-start = ((), (), s32[]{:S(2)}) async-start(), calls=%async_computation.20 | async-start | bytes 8388608
  577.1 281.2 %reduce-scatter.20.cloned.1.call-start = ((), (), s32[]{:S(2)}) async-start(), calls=%async_computation.19 | async-start | bytes 2359296 | tf_op jit(solution)/shard_map/reduce_scatter | solution.py:309
  586.6 310.8 %reduce-scatter.18.cloned.1.call-start = ((), (), s32[]{:S(2)}) async-start(), calls=%async_computation.18 | async-start | bytes 589824 | tf_op jit(solution)/shard_map/reduce_scatter | solution.py:300
  835.2 130.8 %reduce-scatter.16.cloned.1.call-start = ((), (), s32[]{:S(2)}) async-start(), calls=%async_computation.17 | async-start | bytes 1769472 | tf_op jit(solution)/shard_map/reduce_scatter | solution.py:294
  846.5 165.5 %reduce-scatter.14.cloned.1.call-start = ((), (), s32[]{:S(2)}) async-start(), calls=%async_computation.16 | async-start | bytes 5242880 | tf_op jit(solution)/shard_map/reduce_scatter | solution.py:285
  853.6 160.1 %copy-start.50 = (f32[512]{0:T(512)S(1)}, f32[512]{0:T(512)}, u32[]{:S(2)}) copy-start(f32[512]{0:T(512)} %copy-done.49) | copy-start | bytes 6148
  853.6 160.2 %copy-start.46 = (f32[512]{0:T(512)S(1)}, f32[512]{0:T(512)}, u32[]{:S(2)}) copy-start(f32[512]{0:T(512)} %copy-done.45) | copy-start | bytes 6148
  853.6 162.6 %copy-start.51 = (f32[1024]{0:T(1024)S(1)}, f32[1024]{0:T(1024)}, u32[]{:S(2)}) copy-start(f32[1024]{0:T(1024)} %get-tuple-element.261) | copy-start | bytes 12292
  853.7 204.3 %copy-start.44 = (f32[2,1024]{1,0:T(2,128)S(1)}, f32[2,1024]{1,0:T(2,128)}, u32[]{:S(2)}) copy-start(f32[2,1024]{1,0:T(2,128)} %param.37) | copy-start | bytes 24580
  853.7 204.3 %copy-start.52 = (f32[2,1024]{1,0:T(2,128)S(1)}, f32[2,1024]{1,0:T(2,128)}, u32[]{:S(2)}) copy-start(f32[2,1024]{1,0:T(2,128)} %param.38) | copy-start | bytes 24580
  853.7 204.3 %copy-start.53 = (f32[2,1024]{1,0:T(2,128)S(1)}, f32[2,1024]{1,0:T(2,128)}, u32[]{:S(2)}) copy-start(f32[2,1024]{1,0:T(2,128)} %param.39) | copy-start | bytes 24580
  853.7 205.0 %copy-start.7 = (f32[512,1024]{1,0:T(8,128)S(1)}, f32[512,1024]{1,0:T(8,128)}, u32[]{:S(2)}) copy-start(f32[512,1024]{1,0:T(8,128)} %copy-done.6) | copy-start | bytes 6291460
  853.7 205.0 %copy-start.48 = (f32[512]{0:T(512)S(1)}, f32[512]{0:T(512)}, u32[]{:S(2)}) copy-start(f32[512]{0:T(512)} %copy-done.47) | copy-start | bytes 6148
  (67 other events, 908.1 us)
Sparse Core Ops, SparseCore 0:
  21.8 47.4 all-gather.6
  151.0 73.1 reduce-scatter.7
  227.2 73.3 all-gather.10
  302.7 32.7 all-gather.8
  338.2 49.2 all-gather.12
  389.0 32.9 all-gather.14
  454.4 44.5 reduce-scatter.11
  501.5 44.4 reduce-scatter.9
  552.2 34.4 all-gather.16
  590.7 156.3 all-reduce.9
  751.0 66.6 reduce-scatter.19
  835.3 62.0 reduce-scatter.17
  901.4 64.5 reduce-scatter.15
  968.5 43.4 reduce-scatter.13
